TPU v7x, 256 devices: a whole 4x4x8 slice. The times are simulated.
256 devices in a mesh: ctx: 16 (over z_hi, y), head: 16 (over x, z_lo, core).
Axes of the slice: x: 4, y: 4, z: 8 (z_hi: 4, z_lo: 2; z = z_hi * 2 + z_lo), core: 2. Of those that a mesh axis runs over, the one named last changes fastest.
Arguments:
- queries: bfloat16 [4096, 16384], P('ctx', 'head'), may hold values from -10 to 10
- key_states: bfloat16 [4096, 1024], P('ctx'), may hold values from -10 to 10
- value_states: bfloat16 [4096, 1024], P('ctx'), may hold values from -6 to 6
- vertical_blocks: int32 [128, 4], P('head'), may hold values from 0 to 31, as said below
- slash_offsets: int32 [128, 4], P('head'), may hold values from 0 to 31, as said below
- positions: int32 [4096], P('ctx'), may hold values from 0 to 32767, as said below
- out_weight: bfloat16 [16384, 16384], P('head', 'ctx'), may hold values from -0.25 to 0.25
Outputs:
- projected: bfloat16 [4096, 16384], P('head', 'ctx')
Inputs may be any that keep to these rules, and one draw needn't show every extreme that they name: `vertical_blocks`: each head's 4 vertical blocks are distinct. `slash_offsets`: each head's 4 offsets are distinct and the first of them is 0. `positions`: positions rise by one inside each block of 128 tokens; block b starts at a multiple of 128 at or after b * 1024 and before (b + 1) * 1024.
All inputs are finite; a program needn't handle non-finite values.
Results may differ from a plain program's by a relative error of at most 0.025.
Values may be sent and summed in bfloat16 or wider, within the bound.
A program may use at most 64 MiB of HBM per device.

v0:
```python
import math
import jax
import jax.numpy as jnp
from jax import lax
from jax.sharding import PartitionSpec as P

HD = 128
GROUP = 16
BLK = 128


def rotate_heads(states, positions):
    half_width = states.shape[-1] // 2
    exponents = jnp.arange(half_width, dtype=jnp.float32) * (2.0 / states.shape[-1])
    inverse_freq = 500000.0 ** (-exponents)
    angles = positions.astype(jnp.float32)[:, None] * inverse_freq[None, :]
    cosine = jnp.cos(angles)[:, None, :]
    sine_part = jnp.sin(angles)[:, None, :]
    front_half = states[..., :half_width]
    back_half = states[..., half_width:]
    return jnp.concatenate(
        [front_half * cosine - back_half * sine_part, back_half * cosine + front_half * sine_part],
        axis=-1,
    )


def per_device(
    queries, key_states, value_states, vertical_blocks, slash_offsets, positions, out_weight
):
    local_tokens = queries.shape[0]
    local_heads = queries.shape[1] // HD
    head_index = lax.axis_index("head")
    ctx_index = lax.axis_index("ctx")
    shared_head = head_index * local_heads // GROUP
    own_keys = lax.dynamic_slice_in_dim(key_states, shared_head * HD, HD, 1)
    own_values = lax.dynamic_slice_in_dim(value_states, shared_head * HD, HD, 1)
    rotated_own = rotate_heads(own_keys.astype(jnp.float32)[:, None, :], positions)[:, 0, :].astype(
        jnp.bfloat16
    )
    all_keys, all_values = (
        lax.all_gather(rotated_own, "ctx", axis=0, tiled=True),
        lax.all_gather(own_values, "ctx", axis=0, tiled=True),
    )
    query_rot = rotate_heads(
        queries.astype(jnp.float32).reshape(local_tokens, local_heads, HD), positions
    ).astype(jnp.bfloat16)
    query_blocks = local_tokens // BLK
    key_count = all_keys.shape[0] // BLK
    block_ids = ctx_index * query_blocks + jnp.arange(query_blocks, dtype=jnp.int32)
    vert_slots = jnp.broadcast_to(
        vertical_blocks[:, None, :], (local_heads, query_blocks, vertical_blocks.shape[1])
    )
    vert_valid = vert_slots <= block_ids[None, :, None]
    slash_slots = block_ids[None, :, None] - slash_offsets[:, None, :]
    repeated = jnp.any(slash_slots[..., None] == vertical_blocks[:, None, None, :], axis=-1)
    slash_valid = (slash_slots >= 0) & jnp.logical_not(repeated)
    slot_blocks = jnp.concatenate([vert_slots, slash_slots], axis=-1)
    slot_valid = jnp.concatenate([vert_valid, slash_valid], axis=-1)
    safe_blocks = jnp.clip(slot_blocks, 0, key_count - 1)
    key_tiles = all_keys.reshape(key_count, BLK, HD)[safe_blocks]
    value_tiles = all_values.reshape(key_count, BLK, HD)[safe_blocks]
    query_tiles = query_rot.reshape(query_blocks, BLK, local_heads, HD).transpose(2, 0, 1, 3)
    scores = jnp.einsum(
        "hqrd,hqskd->hqrsk", query_tiles, key_tiles, preferred_element_type=jnp.float32
    ) / math.sqrt(HD)
    diagonal = (slot_blocks == block_ids[None, :, None])[:, :, None, :, None]
    causal_pairs = (jnp.arange(BLK)[None, :] <= jnp.arange(BLK)[:, None])[None, None, :, None, :]
    allowed = slot_valid[:, :, None, :, None] & (jnp.logical_not(diagonal) | causal_pairs)
    masked = jnp.where(allowed, scores, -1e30)
    row_max = jnp.max(masked, axis=(3, 4), keepdims=True)
    exponentials = jnp.exp(masked - row_max)
    weights = (exponentials / jnp.sum(exponentials, axis=(3, 4), keepdims=True)).astype(
        jnp.bfloat16
    )
    attended = jnp.einsum(
        "hqrsk,hqskd->hqrd", weights, value_tiles, preferred_element_type=jnp.float32
    ).astype(jnp.bfloat16)
    head_out = attended.transpose(1, 2, 0, 3).reshape(local_tokens, local_heads * HD)
    partial_terms = jnp.dot(
        lax.all_gather(head_out, "ctx", axis=0, tiled=True),
        out_weight,
        preferred_element_type=jnp.float32,
    )
    projected = lax.psum_scatter(
        partial_terms.astype(jnp.bfloat16), "head", scatter_dimension=0, tiled=True
    )
    return projected


def solution(mesh):
    placed = (
        P("ctx", "head"),
        P("ctx", None),
        P("ctx", None),
        P("head", None),
        P("head", None),
        P("ctx"),
        P("head", "ctx"),
    )
    return jax.shard_map(
        per_device, mesh=mesh, in_specs=placed, out_specs=P("head", "ctx"), check_vma=False
    )
```

profile of v0, /device:TPU:8, one launch (start us, length us, event | category | flops | bytes accessed | tf_op | source)
XLA Modules:
  0.0 370.9 jit_solution(2328928914875954693)
XLA Ops:
  6.6 1.0 constant_dynamic-slice_fusion.1
  7.7 0.7 convert_element_type.25
  8.7 0.6 pad_maximum_fusion
  9.4 1.5 constant_dynamic-slice_fusion
  11.0 0.8 broadcast_subtract_fusion
  11.7 0.7 broadcast_in_dim.15
  12.6 0.7 compare_reduce_fusion
  13.3 0.8 broadcast_compare_fusion
  14.2 0.7 broadcast_in_dim.12
  15.0 1.1 convert_bitcast_fusion
  16.4 0.5 multiply_cosine_fusion
  17.3 1.4 subtract_convert_fusion
  18.7 47.3 %all-gather.9.cloned.1.call-done = bf16[4096,1,128]{0,2,1:T(8,128)(2,1)} async-done(((bf16[256,1,128]{0,2,1:T(8,128)(2,1)}), bf16[4096,1,128]{0,2,1:T(8,128)(2,1)}) %all-gather.9.cloned.1.call-update) | async-done | bytes 1048592 | tf_op jit(solution)/shard_map/all_gather | solution.py:41
  66.0 1.6 copy.53
  67.6 3.0 gather_fusion
  70.7 48.9 %all-gather.5.cloned.1.call-done = bf16[4096,128]{1,0:T(8,128)(2,1)} async-done(((bf16[256,128]{1,0:T(8,128)(2,1)}), bf16[4096,128]{1,0:T(8,128)(2,1)}) %all-gather.5.cloned.1.call-update) | async-done | bytes 1048592 | tf_op jit(solution)/shard_map/all_gather | solution.py:42
  119.6 4.4 %gather_fusion.1 = bf16[128,128,128]{2,1,0:T(8,128)(2,1)} fusion(bf16[32,128,128]{2,1,0:T(8,128)(2,1)} %bitcast.44, s32[1024]{0:T(1024)S(1)} %pad_clamp_fusion), kind=kCustom, calls=%fused_computation.1 | custom fusion | bytes 8389120 | tf_op jit(solution)/shard_map/gather | solution.py:61
  124.0 3.9 %fusion.1 = (f32[8,2,128]{2,1,0:T(2,128)S(1)}, f32[8,2,128,8,128]{2,4,3,1,0:T(8,128)S(1)}) fusion(pred[128,128]{0,1:T(8,128)(4,1)S(1)} %iota_compare_fusion, pred[8,2,8]{2,1,0:T(4,128)(4,1)S(1)} %copy.42, pred[8,2,8]{2,1,0:T(4,128)(4,1)S(1)} %copy.41, bf16[8,2,8,128,128]{4,3,2,1,0:T(8,128)(2,1)} %bitcast.47, bf16[2,128,8,64]{3,1,0,2:T(8,128)(2,1)S(1)} %bitcast.51, ...), kind=kOutput, calls=%fused_computation.7 | convolution fusion | flops 548403200 | bytes 13132032 | tf_op jit(solution)/shard_map/hqrd,hqskd->hqrsk/dot_general | solution.py:63
  127.9 3.0 fusion
  130.9 3.9 %fusion.5 = bf16[2,128,8,128]{3,1,0,2:T(8,128)(2,1)S(1)} fusion(bf16[8,2,8,128,128]{4,3,2,1,0:T(8,128)(2,1)S(1)} %bitcast.46, f32[8,2,128,8,128]{2,4,3,1,0:T(8,128)S(1)} %get-tuple-element.18, f32[8,2,128]{2,1,0:T(2,128)S(1)} %fusion, f32[8,2,128]{2,1,0:T(2,128)S(1)} %get-tuple-element.17, pred[128,128]{0,1:T(8,128)(4,1)S(1)} %iota_compare_fusion, ...), kind=kOutput, calls=%fused_computation.11 | convolution fusion | flops 551813120 | bytes 13140224 | tf_op jit(solution)/shard_map/hqrsk,hqskd->hqrd/dot_general | solution.py:75
  135.2 0.9 copy.64
  136.3 101.2 %all-gather.7.cloned.1.call-done = bf16[4096,1024]{1,0:T(8,128)(2,1)} async-done(((bf16[256,1024]{1,0:T(8,128)(2,1)}), bf16[4096,1024]{1,0:T(8,128)(2,1)}) %all-gather.7.cloned.1.call-update) | async-done | bytes 8388624 | tf_op jit(solution)/shard_map/all_gather | solution.py:80
  237.5 14.5 %convolution_convert_fusion = bf16[4096,1024]{1,0:T(8,128)(2,1)} fusion(bf16[4096,1024]{1,0:T(8,128)(2,1)} %all-gather.7.cloned.1.call-done, bf16[1024,1024]{1,0:T(8,128)(2,1)S(1)} %copy-done), kind=kOutput, calls=%fused_computation.5 | convolution fusion | flops 8594128896 | bytes 18874368 | tf_op jit(solution)/shard_map/dot_general | solution.py:79
  252.0 112.3 %reduce-scatter.2.cloned.1.call-done = bf16[256,1024]{1,0:T(8,128)(2,1)} async-done(((bf16[4096,1024]{1,0:T(8,128)(2,1)}), bf16[256,1024]{1,0:T(8,128)(2,1)}) %reduce-scatter.2.cloned.1.call-update) | async-done | bytes 524304 | tf_op jit(solution)/shard_map/reduce_scatter | solution.py:84
  (33 shorter events, 2.2 us)
Async XLA Ops:
  6.5 230.9 %copy-start = (bf16[1024,1024]{1,0:T(8,128)(2,1)S(1)}, bf16[1024,1024]{1,0:T(8,128)(2,1)}, u32[]{:S(2)}) copy-start(bf16[1024,1024]{1,0:T(8,128)(2,1)} %param.13) | copy-start | bytes 6291460
  6.5 59.4 %all-gather.9.cloned.1.call-start = ((), (), s32[]{:S(2)}) async-start(), calls=%async_computation.4 | async-start | bytes 1114112 | tf_op jit(solution)/shard_map/all_gather | solution.py:41
  9.4 110.2 %all-gather.5.cloned.1.call-start = ((), (), s32[]{:S(2)}) async-start(), calls=%async_computation.1 | async-start | bytes 1114112 | tf_op jit(solution)/shard_map/all_gather | solution.py:42
  10.9 226.6 %all-gather.7.cloned.1.call-start = ((), (), s32[]{:S(2)}) async-start(), calls=%async_computation.2 | async-start | bytes 8912896 | tf_op jit(solution)/shard_map/all_gather | solution.py:80
  119.6 4.4 %copy-start.2 = (bf16[256,8,64]{2,0,1:T(8,128)(2,1)S(1)}, bf16[256,8,64]{2,0,1:T(8,128)(2,1)}, u32[]{:S(2)}) copy-start(bf16[256,8,64]{2,0,1:T(8,128)(2,1)} %get-tuple-element.5) | copy-start | bytes 786436
  119.6 4.4 %copy-start.3 = (bf16[256,8,64]{2,0,1:T(8,128)(2,1)S(1)}, bf16[256,8,64]{2,0,1:T(8,128)(2,1)}, u32[]{:S(2)}) copy-start(bf16[256,8,64]{2,0,1:T(8,128)(2,1)} %get-tuple-element.6) | copy-start | bytes 786436
  127.9 3.0 copy-start.1
  136.1 228.3 %reduce-scatter.2.cloned.1.call-start = ((), (), s32[]{:S(2)}) async-start(), calls=%async_computation.3 | async-start | bytes 8912896 | tf_op jit(solution)/shard_map/reduce_scatter | solution.py:84
Sparse Core Ops, SparseCore 0:
  9.8 56.1 all-gather.8
  68.4 51.1 all-gather.4
  136.2 101.2 all-gather.6
  252.1 112.1 reduce-scatter.1
where the time goes:
time: 371 us
  waiting for transfers between devices  310 us (84%)
  matrix products  22.3 us (6%)
  local copies, waits for them, and re-layouts  15.1 us (4%)
  between operations  13.3 us (4%)
  other arithmetic  10.1 us (3%)
    reduce_scatter x1, waiting for transfers between devices, per_device(): lax.psum_scatter(partial_terms.astype(jnp.bfloat16), 'head', scatter_dime...  112 us
    all_gather x1, waiting for transfers between devices, per_device(): lax.all_gather(head_out, 'ctx', axis=0, tiled=True)  101 us
    all_gather x1, waiting for transfers between devices, per_device(): lax.all_gather(own_values, 'ctx', axis=0, tiled=True)  48.9 us
    all_gather x1, waiting for transfers between devices, per_device(): lax.all_gather(rotated_own, 'ctx', axis=0, tiled=True)  47.3 us
    dot_general x1, matrix products, per_device(): jnp.dot(lax.all_gather(head_out, 'ctx', axis=0, tiled=True), out_weight,...  14.5 us
  transfers between devices with their start and end apart: 4, of which 4 were waited for; matrix products, arithmetic and copies ran while one was open for 4% of the time, Pallas kernels for 0%

commit v1 on v0

--- a/solution.py
+++ b/solution.py
@@ -77,7 +77,10 @@
     ).astype(jnp.bfloat16)
     head_out = attended.transpose(1, 2, 0, 3).reshape(local_tokens, local_heads * HD)
     partial_terms = jnp.dot(
-        lax.all_gather(head_out, "ctx", axis=0, tiled=True),
+        jnp.concatenate(
+            lax.all_to_all(jnp.stack([head_out for _ in range(lax.axis_size("ctx"))]), "ctx", 0, 0),
+            axis=0,
+        ),
         out_weight,
         preferred_element_type=jnp.float32,
     )

time: 371 us -> 442 us (1.19)
  blocking collectives: 0 us -> 148 us
  waiting for transfers between devices: 310 us -> 237 us
    all_to_all x0 -> x1, blocking collectives: none -> 148 us  [per_device(): lax.all_to_all(jnp.stack([head_out for _ in range(lax.axis_size('ctx'))])...]
    all_gather x1 -> x0, waiting for transfers between devices: 101 us -> none  [per_device(): lax.all_gather(head_out, 'ctx', axis=0, tiled=True)]
    reduce_scatter x1, waiting for transfers between devices: 112 us -> 141 us  [per_device(): lax.psum_scatter(partial_terms.astype(jnp.bfloat16), 'head', scatter_dime...]
  transfers between devices with their start and end apart: 4 -> 3, of which waited for: 4 -> 3; matrix products, arithmetic and copies ran while one was open for 4% -> 3% of each run, Pallas kernels for 0% -> 0%
where the time goes in v1:
time: 442 us
  waiting for transfers between devices  237 us (54%)
  blocking collectives  148 us (33%)
  matrix products  18.6 us (4%)
  local copies, waits for them, and re-layouts  15.4 us (3%)
  between operations  13.3 us (3%)
  other arithmetic  10.1 us (2%)
    all_to_all x1, blocking collectives, per_device(): lax.all_to_all(jnp.stack([head_out for _ in range(lax.axis_size('ctx'))])...  148 us
    reduce_scatter x1, waiting for transfers between devices, per_device(): lax.psum_scatter(partial_terms.astype(jnp.bfloat16), 'head', scatter_dime...  141 us
    all_gather x1, waiting for transfers between devices, per_device(): lax.all_gather(own_values, 'ctx', axis=0, tiled=True)  49 us
    all_gather x1, waiting for transfers between devices, per_device(): lax.all_gather(rotated_own, 'ctx', axis=0, tiled=True)  47.3 us
    dot_general x1, matrix products, per_device(): jnp.dot(jnp.concatenate(lax.all_to_all(jnp.stack([head_out for _ in range...  10.8 us
  transfers between devices with their start and end apart: 3, of which 3 were waited for; matrix products, arithmetic and copies ran while one was open for 3% of the time, Pallas kernels for 0%

profile of v1, /device:TPU:8, one launch (start us, length us, event | category | flops | bytes accessed | tf_op | source)
XLA Modules:
  0.0 441.9 jit_solution(9192286568672439561)
XLA Ops:
  6.6 1.0 constant_dynamic-slice_fusion.1
  7.7 0.7 convert_element_type.25
  8.7 0.6 pad_maximum_fusion
  9.4 1.5 constant_dynamic-slice_fusion
  11.0 0.8 broadcast_subtract_fusion
  11.7 0.7 broadcast_in_dim.15
  12.6 0.7 compare_reduce_fusion
  13.3 0.8 broadcast_compare_fusion
  14.2 0.7 broadcast_in_dim.12
  15.1 1.1 convert_bitcast_fusion
  16.4 0.5 multiply_cosine_fusion
  17.3 1.4 subtract_convert_fusion
  18.7 47.3 %all-gather.6.cloned.1.call-done = bf16[4096,1,128]{0,2,1:T(8,128)(2,1)} async-done(((bf16[256,1,128]{0,2,1:T(8,128)(2,1)}), bf16[4096,1,128]{0,2,1:T(8,128)(2,1)}) %all-gather.6.cloned.1.call-update) | async-done | bytes 1048592 | tf_op jit(solution)/shard_map/all_gather | solution.py:41
  66.0 1.6 copy.53
  67.6 3.0 gather_fusion
  70.6 49.0 %all-gather.4.cloned.1.call-done = bf16[4096,128]{1,0:T(8,128)(2,1)} async-done(((bf16[256,128]{1,0:T(8,128)(2,1)}), bf16[4096,128]{1,0:T(8,128)(2,1)}) %all-gather.4.cloned.1.call-update) | async-done | bytes 1048592 | tf_op jit(solution)/shard_map/all_gather | solution.py:42
  119.6 4.4 gather_fusion.1
  124.0 3.9 fusion.1
  127.9 3.0 fusion
  130.9 3.8 fusion.5
  135.2 1.1 stack.3
  136.3 147.6 %all_to_all.5 = bf16[16,256,1024]{2,1,0:T(8,128)(2,1)S(1)} all-to-all(bf16[16,256,1024]{2,1,0:T(8,128)(2,1)S(1)} %stack.3), channel_id=1, replica_groups=mesh['ctx'=16,'head'=16] {'ctx'}, dimensions={0} | all-to-all | bytes 16777216 | tf_op jit(solution)/shard_map/all_to_all | solution.py:81
  284.0 10.8 %convolution_convert_fusion = bf16[4096,1024]{1,0:T(8,128)(2,1)} fusion(bf16[4096,1024]{1,0:T(8,128)(2,1)S(1)} %bitcast.47, bf16[1024,1024]{1,0:T(8,128)(2,1)S(1)} %copy-done), kind=kOutput, calls=%fused_computation.5 | convolution fusion | flops 8594128896 | bytes 18874368 | tf_op jit(solution)/shard_map/dot_general | solution.py:79
  294.8 140.6 %reduce-scatter.2.cloned.1.call-done = bf16[256,1024]{1,0:T(8,128)(2,1)} async-done(((bf16[4096,1024]{1,0:T(8,128)(2,1)}), bf16[256,1024]{1,0:T(8,128)(2,1)}) %reduce-scatter.2.cloned.1.call-update) | async-done | bytes 524304 | tf_op jit(solution)/shard_map/reduce_scatter | solution.py:87
  (32 shorter events, 2.1 us)
Async XLA Ops:
  6.5 277.4 %copy-start = (bf16[1024,1024]{1,0:T(8,128)(2,1)S(1)}, bf16[1024,1024]{1,0:T(8,128)(2,1)}, u32[]{:S(2)}) copy-start(bf16[1024,1024]{1,0:T(8,128)(2,1)} %param.13) | copy-start | bytes 6291460
  6.5 59.4 %all-gather.6.cloned.1.call-start = ((), (), s32[]{:S(2)}) async-start(), calls=%async_computation.4 | async-start | bytes 1114112 | tf_op jit(solution)/shard_map/all_gather | solution.py:41
  9.4 110.2 %all-gather.4.cloned.1.call-start = ((), (), s32[]{:S(2)}) async-start(), calls=%async_computation.2 | async-start | bytes 1114112 | tf_op jit(solution)/shard_map/all_gather | solution.py:42
  10.9 424.5 %reduce-scatter.2.cloned.1.call-start = ((), (), s32[]{:S(2)}) async-start(), calls=%async_computation.3 | async-start | bytes 8912896 | tf_op jit(solution)/shard_map/reduce_scatter | solution.py:87
  119.6 4.4 copy-start.2
  119.6 4.4 copy-start.3
  127.9 3.1 copy-start.1
Sparse Core Ops, SparseCore 0:
  9.8 56.1 all-gather.5
  68.4 51.1 all-gather.3
  294.9 140.4 reduce-scatter.1
